TPU v7x, 256 devices: a whole 4x4x8 slice. The times are simulated.
256 devices in a mesh: row: 16 (over z, core), col: 16 (over y, x).
Axes of the slice: x: 4, y: 4, z: 8, core: 2. Of those that a mesh axis runs over, the one named last changes fastest.
Arguments:
- sigma_anc: float32 [48, 48, 128, 128], P('row', 'col'), as said below
- factor: float32 [16, 256, 128, 128], P('row', 'col'), may hold values from -1.25 to 1.25
- diag_inv: float32 [256, 128, 128], P('col'), as said below
- struct: int32 [256, 16], P('col'), may hold values from 0 to 47, all different within a row
Outputs:
- z_off: float32 [256, 48, 128, 128], P('col', 'row')
- z_diag: float32 [256, 128, 128], P(('col', 'row'))
Inputs may be any that keep to these rules, and one draw needn't show every extreme that they name: Each row of struct names 16 different ancestor blocks, and every ancestor block is named by some row. sigma_anc is symmetric: block [b, a] is the transpose of block [a, b]. Each diag_inv[k] is lower triangular with a positive diagonal.
All inputs are finite; a program needn't handle non-finite values.
Results may differ from a plain program's by a relative error of at most 0.0003.
Values sent between devices are 32-bit elements; how exact they have to be, the bound alone decides.
A program may use at most 128 MiB of HBM per device.

v0:
```python
import jax
import jax.numpy as jnp
from jax import lax
from jax.sharding import PartitionSpec as P

highest = lax.Precision.HIGHEST


def select_blocks(sigma_rows, slot_ids):
    return jnp.take(sigma_rows, slot_ids, axis=1)


def body(sigma_anc, factor, diag_inv, struct):
    row_count = sigma_anc.shape[0]
    node_count = diag_inv.shape[0]
    width = diag_inv.shape[1]
    row_index = lax.axis_index("row")
    own_rows = row_index * row_count + jnp.arange(row_count, dtype=jnp.int32)
    sigma_rows = lax.all_gather(sigma_anc, "col", axis=1, tiled=True)
    u_local = jnp.einsum("skij,kjl->skil", factor, diag_inv, precision=highest)
    empty = jnp.zeros((node_count, row_count, width, width), jnp.float32)

    def one_slot(running, element):
        u_slot, id_slot = element
        y_sum, u_rows = running
        picked = select_blocks(sigma_rows, id_slot)
        y_sum = y_sum + jnp.einsum("akij,kjl->kail", picked, u_slot, precision=highest)
        match = (id_slot[:, None] == own_rows[None, :]).astype(jnp.float32)
        u_rows = u_rows + match[:, :, None, None] * u_slot[:, None, :, :]
        return ((y_sum, u_rows), None)

    result, unused_out = lax.scan(
        one_slot,
        (empty, empty),
        (lax.all_gather(u_local, "row", axis=0, tiled=True), jnp.transpose(struct)),
    )
    y_rows, u_rows = result
    member = jnp.any(struct[:, :, None] == own_rows[None, None, :], axis=1)
    z_off = jnp.where(member[:, :, None, None], -y_rows, 0.0)
    partial_sum = jnp.einsum("kaij,kail->kjl", u_rows, y_rows, precision=highest)
    share_count = node_count // lax.axis_size("row")
    start_node = row_index * share_count
    inverse_share = lax.dynamic_slice_in_dim(diag_inv, start_node, share_count, 0)
    inverse_part = jnp.einsum("kij,kil->kjl", inverse_share, inverse_share, precision=highest)
    summed = lax.psum(partial_sum, "row")
    mine = lax.dynamic_slice_in_dim(summed, start_node, share_count, 0)
    return (z_off, inverse_part + mine)


def solution(mesh):
    in_specs = (
        P("row", "col", None, None),
        P("row", "col", None, None),
        P("col", None, None),
        P("col", None),
    )
    out_specs = (P("col", "row", None, None), P(("col", "row"), None, None))
    return jax.shard_map(body, mesh=mesh, in_specs=in_specs, out_specs=out_specs, check_vma=False)
```

profile of v0, /device:TPU:1, one launch (start us, length us, event | category | flops | bytes accessed | tf_op | source)
XLA Modules:
  0.0 607.2 jit_solution(9201970120801829042)
XLA Ops:
  13.0 82.0 %all-gather.3.cloned.1.call-done = f32[3,48,128,128]{3,2,1,0:T(8,128)} async-done(((f32[3,3,128,128]{3,2,1,0:T(8,128)}), f32[3,48,128,128]{3,2,1,0:T(8,128)}) %all-gather.3.cloned.1.call-update) | async-done | bytes 9437200 | tf_op jit(solution)/shard_map/all_gather | solution.py:19
  95.0 97.4 %all-gather.5.cloned.1.call-done = f32[16,16,128,128]{3,2,1,0:T(8,128)} async-done(((f32[1,16,128,128]{3,2,1,0:T(8,128)}), f32[16,16,128,128]{3,2,1,0:T(8,128)}) %all-gather.5.cloned.1.call-update) | async-done | bytes 16777232 | tf_op jit(solution)/shard_map/all_gather | solution.py:35
  192.4 287.7 %while.13 = (s32[]{:T(128)}, f32[16,3,128,128]{3,2,1,0:T(8,128)}, f32[16,3,128,128]{3,2,1,0:T(8,128)}, s32[16,16]{1,0:T(8,128)S(1)}, f32[3,48,128,128]{3,2,1,0:T...) while((s32[]{:T(128)}, f32[16,3,128,128]{3,2,1,0:T(8,128)}, ...), condition=%wide.region_2.3_spmd.clone, body=%wide.region_1.2_spmd.clone.sunk | while | flops 1212679424 | bytes 26220016 | solution.py:32
  192.5 6.1 gather_fusion
  198.5 6.2 %select_add_fusion.4 = f32[16,3,128,128]{3,2,1,0:T(8,128)} fusion(f32[16,3,128,128]{3,2,1,0:T(8,128)} %get-tuple-element.149, f32[16,3,128,128]{3,2,1,0:T(8,128)} %gather_fusion, pred[16]{0:T(512)(128)(4,1)S(1)} %get-tuple-element.137, pred[]{:T(512)S(6)} %compare.3, f32[16,16,128,128]{3,2,1,0:T(8,128)} %get-tuple-element.162, s32[]{:T(128)} %get-tuple-element.148), kind=kOutput, calls=%fused_computation.5.clone.1 | convolution fusion | flops 1210318848 | bytes 10486289 | tf_op jit(solution)/shard_map/while/body/eval_jaxpr/akij,kjl->kail/dot_general | solution.py:27
  208.2 6.1 gather_fusion
  214.3 6.7 %select_add_fusion.4 = f32[16,3,128,128]{3,2,1,0:T(8,128)} fusion(f32[16,3,128,128]{3,2,1,0:T(8,128)} %get-tuple-element.149, f32[16,3,128,128]{3,2,1,0:T(8,128)} %gather_fusion, pred[16]{0:T(512)(128)(4,1)S(1)} %get-tuple-element.137, pred[]{:T(512)S(6)} %compare.3, f32[16,16,128,128]{3,2,1,0:T(8,128)} %get-tuple-element.162, s32[]{:T(128)} %get-tuple-element.148), kind=kOutput, calls=%fused_computation.5.clone.1 | convolution fusion | flops 1210318848 | bytes 10486289 | tf_op jit(solution)/shard_map/while/body/eval_jaxpr/akij,kjl->kail/dot_general | solution.py:27
  226.4 6.1 gather_fusion
  232.4 6.7 %select_add_fusion.4 = f32[16,3,128,128]{3,2,1,0:T(8,128)} fusion(f32[16,3,128,128]{3,2,1,0:T(8,128)} %get-tuple-element.149, f32[16,3,128,128]{3,2,1,0:T(8,128)} %gather_fusion, pred[16]{0:T(512)(128)(4,1)S(1)} %get-tuple-element.137, pred[]{:T(512)S(6)} %compare.3, f32[16,16,128,128]{3,2,1,0:T(8,128)} %get-tuple-element.162, s32[]{:T(128)} %get-tuple-element.148), kind=kOutput, calls=%fused_computation.5.clone.1 | convolution fusion | flops 1210318848 | bytes 10486289 | tf_op jit(solution)/shard_map/while/body/eval_jaxpr/akij,kjl->kail/dot_general | solution.py:27
  250.6 6.7 %select_add_fusion.4 = f32[16,3,128,128]{3,2,1,0:T(8,128)} fusion(f32[16,3,128,128]{3,2,1,0:T(8,128)} %get-tuple-element.149, f32[16,3,128,128]{3,2,1,0:T(8,128)} %gather_fusion, pred[16]{0:T(512)(128)(4,1)S(1)} %get-tuple-element.137, pred[]{:T(512)S(6)} %compare.3, f32[16,16,128,128]{3,2,1,0:T(8,128)} %get-tuple-element.162, s32[]{:T(128)} %get-tuple-element.148), kind=kOutput, calls=%fused_computation.5.clone.1 | convolution fusion | flops 1210318848 | bytes 10486289 | tf_op jit(solution)/shard_map/while/body/eval_jaxpr/akij,kjl->kail/dot_general | solution.py:27
  268.7 6.7 %select_add_fusion.4 = f32[16,3,128,128]{3,2,1,0:T(8,128)} fusion(f32[16,3,128,128]{3,2,1,0:T(8,128)} %get-tuple-element.149, f32[16,3,128,128]{3,2,1,0:T(8,128)} %gather_fusion, pred[16]{0:T(512)(128)(4,1)S(1)} %get-tuple-element.137, pred[]{:T(512)S(6)} %compare.3, f32[16,16,128,128]{3,2,1,0:T(8,128)} %get-tuple-element.162, s32[]{:T(128)} %get-tuple-element.148), kind=kOutput, calls=%fused_computation.5.clone.1 | convolution fusion | flops 1210318848 | bytes 10486289 | tf_op jit(solution)/shard_map/while/body/eval_jaxpr/akij,kjl->kail/dot_general | solution.py:27
  286.8 6.7 %select_add_fusion.4 = f32[16,3,128,128]{3,2,1,0:T(8,128)} fusion(f32[16,3,128,128]{3,2,1,0:T(8,128)} %get-tuple-element.149, f32[16,3,128,128]{3,2,1,0:T(8,128)} %gather_fusion, pred[16]{0:T(512)(128)(4,1)S(1)} %get-tuple-element.137, pred[]{:T(512)S(6)} %compare.3, f32[16,16,128,128]{3,2,1,0:T(8,128)} %get-tuple-element.162, s32[]{:T(128)} %get-tuple-element.148), kind=kOutput, calls=%fused_computation.5.clone.1 | convolution fusion | flops 1210318848 | bytes 10486289 | tf_op jit(solution)/shard_map/while/body/eval_jaxpr/akij,kjl->kail/dot_general | solution.py:27
  305.0 6.7 %select_add_fusion.4 = f32[16,3,128,128]{3,2,1,0:T(8,128)} fusion(f32[16,3,128,128]{3,2,1,0:T(8,128)} %get-tuple-element.149, f32[16,3,128,128]{3,2,1,0:T(8,128)} %gather_fusion, pred[16]{0:T(512)(128)(4,1)S(1)} %get-tuple-element.137, pred[]{:T(512)S(6)} %compare.3, f32[16,16,128,128]{3,2,1,0:T(8,128)} %get-tuple-element.162, s32[]{:T(128)} %get-tuple-element.148), kind=kOutput, calls=%fused_computation.5.clone.1 | convolution fusion | flops 1210318848 | bytes 10486289 | tf_op jit(solution)/shard_map/while/body/eval_jaxpr/akij,kjl->kail/dot_general | solution.py:27
  323.1 6.7 %select_add_fusion.4 = f32[16,3,128,128]{3,2,1,0:T(8,128)} fusion(f32[16,3,128,128]{3,2,1,0:T(8,128)} %get-tuple-element.149, f32[16,3,128,128]{3,2,1,0:T(8,128)} %gather_fusion, pred[16]{0:T(512)(128)(4,1)S(1)} %get-tuple-element.137, pred[]{:T(512)S(6)} %compare.3, f32[16,16,128,128]{3,2,1,0:T(8,128)} %get-tuple-element.162, s32[]{:T(128)} %get-tuple-element.148), kind=kOutput, calls=%fused_computation.5.clone.1 | convolution fusion | flops 1210318848 | bytes 10486289 | tf_op jit(solution)/shard_map/while/body/eval_jaxpr/akij,kjl->kail/dot_general | solution.py:27
  341.2 6.7 %select_add_fusion.4 = f32[16,3,128,128]{3,2,1,0:T(8,128)} fusion(f32[16,3,128,128]{3,2,1,0:T(8,128)} %get-tuple-element.149, f32[16,3,128,128]{3,2,1,0:T(8,128)} %gather_fusion, pred[16]{0:T(512)(128)(4,1)S(1)} %get-tuple-element.137, pred[]{:T(512)S(6)} %compare.3, f32[16,16,128,128]{3,2,1,0:T(8,128)} %get-tuple-element.162, s32[]{:T(128)} %get-tuple-element.148), kind=kOutput, calls=%fused_computation.5.clone.1 | convolution fusion | flops 1210318848 | bytes 10486289 | tf_op jit(solution)/shard_map/while/body/eval_jaxpr/akij,kjl->kail/dot_general | solution.py:27
  359.4 6.7 %select_add_fusion.4 = f32[16,3,128,128]{3,2,1,0:T(8,128)} fusion(f32[16,3,128,128]{3,2,1,0:T(8,128)} %get-tuple-element.149, f32[16,3,128,128]{3,2,1,0:T(8,128)} %gather_fusion, pred[16]{0:T(512)(128)(4,1)S(1)} %get-tuple-element.137, pred[]{:T(512)S(6)} %compare.3, f32[16,16,128,128]{3,2,1,0:T(8,128)} %get-tuple-element.162, s32[]{:T(128)} %get-tuple-element.148), kind=kOutput, calls=%fused_computation.5.clone.1 | convolution fusion | flops 1210318848 | bytes 10486289 | tf_op jit(solution)/shard_map/while/body/eval_jaxpr/akij,kjl->kail/dot_general | solution.py:27
  377.5 6.7 %select_add_fusion.4 = f32[16,3,128,128]{3,2,1,0:T(8,128)} fusion(f32[16,3,128,128]{3,2,1,0:T(8,128)} %get-tuple-element.149, f32[16,3,128,128]{3,2,1,0:T(8,128)} %gather_fusion, pred[16]{0:T(512)(128)(4,1)S(1)} %get-tuple-element.137, pred[]{:T(512)S(6)} %compare.3, f32[16,16,128,128]{3,2,1,0:T(8,128)} %get-tuple-element.162, s32[]{:T(128)} %get-tuple-element.148), kind=kOutput, calls=%fused_computation.5.clone.1 | convolution fusion | flops 1210318848 | bytes 10486289 | tf_op jit(solution)/shard_map/while/body/eval_jaxpr/akij,kjl->kail/dot_general | solution.py:27
  395.6 6.7 %select_add_fusion.4 = f32[16,3,128,128]{3,2,1,0:T(8,128)} fusion(f32[16,3,128,128]{3,2,1,0:T(8,128)} %get-tuple-element.149, f32[16,3,128,128]{3,2,1,0:T(8,128)} %gather_fusion, pred[16]{0:T(512)(128)(4,1)S(1)} %get-tuple-element.137, pred[]{:T(512)S(6)} %compare.3, f32[16,16,128,128]{3,2,1,0:T(8,128)} %get-tuple-element.162, s32[]{:T(128)} %get-tuple-element.148), kind=kOutput, calls=%fused_computation.5.clone.1 | convolution fusion | flops 1210318848 | bytes 10486289 | tf_op jit(solution)/shard_map/while/body/eval_jaxpr/akij,kjl->kail/dot_general | solution.py:27
  413.8 6.7 %select_add_fusion.4 = f32[16,3,128,128]{3,2,1,0:T(8,128)} fusion(f32[16,3,128,128]{3,2,1,0:T(8,128)} %get-tuple-element.149, f32[16,3,128,128]{3,2,1,0:T(8,128)} %gather_fusion, pred[16]{0:T(512)(128)(4,1)S(1)} %get-tuple-element.137, pred[]{:T(512)S(6)} %compare.3, f32[16,16,128,128]{3,2,1,0:T(8,128)} %get-tuple-element.162, s32[]{:T(128)} %get-tuple-element.148), kind=kOutput, calls=%fused_computation.5.clone.1 | convolution fusion | flops 1210318848 | bytes 10486289 | tf_op jit(solution)/shard_map/while/body/eval_jaxpr/akij,kjl->kail/dot_general | solution.py:27
  431.9 6.7 %select_add_fusion.4 = f32[16,3,128,128]{3,2,1,0:T(8,128)} fusion(f32[16,3,128,128]{3,2,1,0:T(8,128)} %get-tuple-element.149, f32[16,3,128,128]{3,2,1,0:T(8,128)} %gather_fusion, pred[16]{0:T(512)(128)(4,1)S(1)} %get-tuple-element.137, pred[]{:T(512)S(6)} %compare.3, f32[16,16,128,128]{3,2,1,0:T(8,128)} %get-tuple-element.162, s32[]{:T(128)} %get-tuple-element.148), kind=kOutput, calls=%fused_computation.5.clone.1 | convolution fusion | flops 1210318848 | bytes 10486289 | tf_op jit(solution)/shard_map/while/body/eval_jaxpr/akij,kjl->kail/dot_general | solution.py:27
  450.0 6.7 %select_add_fusion.4 = f32[16,3,128,128]{3,2,1,0:T(8,128)} fusion(f32[16,3,128,128]{3,2,1,0:T(8,128)} %get-tuple-element.149, f32[16,3,128,128]{3,2,1,0:T(8,128)} %gather_fusion, pred[16]{0:T(512)(128)(4,1)S(1)} %get-tuple-element.137, pred[]{:T(512)S(6)} %compare.3, f32[16,16,128,128]{3,2,1,0:T(8,128)} %get-tuple-element.162, s32[]{:T(128)} %get-tuple-element.148), kind=kOutput, calls=%fused_computation.5.clone.1 | convolution fusion | flops 1210318848 | bytes 10486289 | tf_op jit(solution)/shard_map/while/body/eval_jaxpr/akij,kjl->kail/dot_general | solution.py:27
  468.2 6.7 %select_add_fusion.4 = f32[16,3,128,128]{3,2,1,0:T(8,128)} fusion(f32[16,3,128,128]{3,2,1,0:T(8,128)} %get-tuple-element.149, f32[16,3,128,128]{3,2,1,0:T(8,128)} %gather_fusion, pred[16]{0:T(512)(128)(4,1)S(1)} %get-tuple-element.137, pred[]{:T(512)S(6)} %compare.3, f32[16,16,128,128]{3,2,1,0:T(8,128)} %get-tuple-element.162, s32[]{:T(128)} %get-tuple-element.148), kind=kOutput, calls=%fused_computation.5.clone.1 | convolution fusion | flops 1210318848 | bytes 10486289 | tf_op jit(solution)/shard_map/while/body/eval_jaxpr/akij,kjl->kail/dot_general | solution.py:27
  480.2 9.0 %convolution_bitcast_fusion = f32[16,128,128]{2,1,0:T(8,128)} fusion(f32[16,3,128,128]{3,2,1,0:T(8,128)} %get-tuple-element.41, f32[16,3,128,128]{3,2,1,0:T(8,128)} %get-tuple-element.40), kind=kOutput, calls=%fused_computation.24 | convolution fusion | flops 1207959552 | bytes 7340032 | tf_op jit(solution)/shard_map/kaij,kail->kjl/dot_general | solution.py:40
  493.4 105.4 %all-reduce.2.cloned.1.call-done = f32[16,128,128]{2,1,0:T(8,128)} async-done(((f32[16,128,128]{2,1,0:T(8,128)}), f32[16,128,128]{2,1,0:T(8,128)}) %all-reduce.2.cloned.1.call-update) | async-done | bytes 1048592 | tf_op jit(solution)/shard_map/psum | solution.py:45
  (145 shorter events, 174.5 us)
Async XLA Ops:
  7.2 1.2 copy-start
  7.2 87.8 %all-gather.3.cloned.1.call-start = ((), (), s32[]{:S(2)}) async-start(), calls=%async_computation | async-start | bytes 10027008 | tf_op jit(solution)/shard_map/all_gather | solution.py:19
  7.9 5.0 copy-start.1
  7.9 184.5 %all-gather.5.cloned.1.call-start = ((), (), s32[]{:S(2)}) async-start(), calls=%async_computation.1 | async-start | bytes 17825792 | tf_op jit(solution)/shard_map/all_gather | solution.py:35
  12.8 586.0 %all-reduce.2.cloned.1.call-start = ((), (), s32[]{:S(2)}) async-start(), calls=%async_computation.2 | async-start | bytes 2097152 | tf_op jit(solution)/shard_map/psum | solution.py:45
Sparse Core Ops, SparseCore 0:
  10.4 84.5 all-gather.2
  96.8 95.5 all-gather.4
  489.3 109.5 all-reduce.1
where the time goes:
time: 609 us; the launch traced here: 607 us
  waiting for transfers between devices  286 us (47%)
  local copies, waits for them, and re-layouts  120 us (20%)
  matrix products  120 us (20%)
  other arithmetic  67.3 us (11%)
  between operations  13.8 us (2%)
    dot_general x16, matrix products, one_slot(): jnp.einsum('akij,kjl->kail', picked, u_slot, precision=highest)  106 us
    psum x1, waiting for transfers between devices, body(): summed = lax.psum(partial_sum, 'row')  105 us
    all_gather x1, waiting for transfers between devices, body(): lax.all_gather(u_local, 'row', axis=0, tiled=True)  97.4 us
    gather x16, local copies, waits for them, and re-layouts, select_blocks(): return jnp.take(sigma_rows, slot_ids, axis=1)  97.1 us
    all_gather x1, waiting for transfers between devices, body(): sigma_rows = lax.all_gather(sigma_anc, 'col', axis=1, tiled=True)  82 us
    add x16, other arithmetic, one_slot(): u_rows = u_rows + match[:, :, None, None] * u_slot[:, None, :, :]  61.5 us
    squeeze x16, local copies, waits for them, and re-layouts, body(): lax.scan(one_slot, (empty, empty), (lax.all_gather(u_local, 'row', axis=0...  20.7 us
  transfers between devices with their start and end apart: 3, of which 3 were waited for; matrix products, arithmetic and copies ran while one was open for 1% of the time, Pallas kernels for 0%

commit v1 on v0

--- a/solution.py
+++ b/solution.py
@@ -16,7 +16,21 @@
     width = diag_inv.shape[1]
     row_index = lax.axis_index("row")
     own_rows = row_index * row_count + jnp.arange(row_count, dtype=jnp.int32)
-    sigma_rows = lax.all_gather(sigma_anc, "col", axis=1, tiled=True)
+    ways, here, step = (lax.axis_size("col"), lax.axis_index("col"), sigma_anc.shape[1])
+    dims = [n * ways if d == 1 else n for d, n in enumerate(sigma_anc.shape)]
+    full = lax.dynamic_update_slice_in_dim(
+        jnp.zeros(dims, sigma_anc.dtype), sigma_anc, here * step, axis=1
+    )
+    going_up = going_down = sigma_anc
+    for far in range(1, ways // 2 + 1):
+        going_up = lax.ppermute(going_up, "col", [(d, (d + 1) % ways) for d in range(ways)])
+        full = lax.dynamic_update_slice_in_dim(full, going_up, (here - far) % ways * step, axis=1)
+        if 2 * far < ways:
+            going_down = lax.ppermute(going_down, "col", [(d, (d - 1) % ways) for d in range(ways)])
+            full = lax.dynamic_update_slice_in_dim(
+                full, going_down, (here + far) % ways * step, axis=1
+            )
+    sigma_rows = full
     u_local = jnp.einsum("skij,kjl->skil", factor, diag_inv, precision=highest)
     empty = jnp.zeros((node_count, row_count, width, width), jnp.float32)
 

time: 609 us -> 560 us (0.920)
  waiting for transfers between devices: 286 us -> 176 us
  starting transfers between devices: 0.12 us -> 35.3 us
  local copies, waits for them, and re-layouts: 120 us -> 143 us
    all_gather x1, waiting for transfers between devices: 97.4 us -> 0.01 us  [body(): lax.all_gather(u_local, 'row', axis=0, tiled=True)]
    all_gather x1 -> x0, waiting for transfers between devices: 82 us -> none  [body(): sigma_rows = lax.all_gather(sigma_anc, 'col', axis=1, tiled=True)]
    ppermute x0 -> x15, waiting for transfers between devices: none -> 55.2 us  [the longest x8 51.2 us: body(): lax.ppermute(going_up, 'col', [(d, (d + 1) % ways) for d in range(ways)])]
    ppermute x0 -> x15, starting transfers between devices: none -> 35.2 us  [the longest x7 33.1 us: body(): lax.ppermute(going_down, 'col', [(d, (d - 1) % ways) for d in range(ways)])]
    dynamic_update_slice x0 -> x16, local copies, waits for them, and re-layouts: none -> 17.2 us  [the longest x8 9.08 us: body(): lax.dynamic_update_slice_in_dim(full, going_up, (here - far) % ways * ste...]
    psum x1, waiting for transfers between devices: 105 us -> 120 us  [body(): summed = lax.psum(partial_sum, 'row')]
  transfers between devices with their start and end apart: 3 -> 17, of which waited for: 3 -> 9; matrix products, arithmetic and copies ran while one was open for 1% -> 5% of each run, Pallas kernels for 0% -> 0%
where the time goes in v1:
time: 560 us; the launch traced here: 557 us
  waiting for transfers between devices  176 us (31%)
  local copies, waits for them, and re-layouts  143 us (26%)
  matrix products  120 us (21%)
  other arithmetic  68.2 us (12%)
  starting transfers between devices  35.3 us (6%)
  between operations  14.2 us (3%)
    psum x1, waiting for transfers between devices, body(): summed = lax.psum(partial_sum, 'row')  120 us
    dot_general x16, matrix products, one_slot(): jnp.einsum('akij,kjl->kail', picked, u_slot, precision=highest)  107 us
    gather x16, local copies, waits for them, and re-layouts, select_blocks(): return jnp.take(sigma_rows, slot_ids, axis=1)  97.3 us
    add x16, other arithmetic, one_slot(): u_rows = u_rows + match[:, :, None, None] * u_slot[:, None, :, :]  62.4 us
    ppermute x8, waiting for transfers between devices, body(): lax.ppermute(going_up, 'col', [(d, (d + 1) % ways) for d in range(ways)])  51.2 us
    ppermute x7, starting transfers between devices, body(): lax.ppermute(going_down, 'col', [(d, (d - 1) % ways) for d in range(ways)])  33.1 us
    squeeze x16, local copies, waits for them, and re-layouts, body(): lax.scan(one_slot, (empty, empty), (lax.all_gather(u_local, 'row', axis=0...  20.7 us
  transfers between devices with their start and end apart: 17, of which 9 were waited for; matrix products, arithmetic and copies ran while one was open for 5% of the time, Pallas kernels for 0%

profile of v1, /device:TPU:1, one launch (start us, length us, event | category | flops | bytes accessed | tf_op | source)
XLA Modules:
  0.0 557.4 jit_solution(12089556227682561473)
XLA Ops:
  18.8 11.2 %collective-permute-done = f32[3,3,128,128]{3,2,1,0:T(8,128)S(1)} collective-permute-done((f32[3,3,128,128]{3,2,1,0:T(8,128)}, f32[3,3,128,128]{3,2,1,0:T(8,128)S(1)}, u32[]{:S(2)}, u32[]{:S(2)}) %collective-permute-start) | collective-permute-done | bytes 589856 | tf_op jit(solution)/shard_map/ppermute | solution.py:26
  34.8 10.2 %collective-permute-done.2 = f32[3,3,128,128]{3,2,1,0:T(8,128)S(1)} collective-permute-done((f32[3,3,128,128]{3,2,1,0:T(8,128)S(1)}, f32[3,3,128,128]{3,2,1,0:T(8,128)S(1)}, u32[]{:S(2)}, u32[]{:S(2)}) %collective-permute-start.2) | collective-permute-done | bytes 589856 | tf_op jit(solution)/shard_map/ppermute | solution.py:26
  49.9 9.2 %collective-permute-done.4 = f32[3,3,128,128]{3,2,1,0:T(8,128)S(1)} collective-permute-done((f32[3,3,128,128]{3,2,1,0:T(8,128)S(1)}, f32[3,3,128,128]{3,2,1,0:T(8,128)S(1)}, u32[]{:S(2)}, u32[]{:S(2)}) %collective-permute-start.4) | collective-permute-done | bytes 589856 | tf_op jit(solution)/shard_map/ppermute | solution.py:26
  63.8 8.4 %collective-permute-done.6 = f32[3,3,128,128]{3,2,1,0:T(8,128)} collective-permute-done((f32[3,3,128,128]{3,2,1,0:T(8,128)S(1)}, f32[3,3,128,128]{3,2,1,0:T(8,128)}, u32[]{:S(2)}, u32[]{:S(2)}) %collective-permute-start.6) | collective-permute-done | bytes 589856 | tf_op jit(solution)/shard_map/ppermute | solution.py:26
  77.9 6.7 %collective-permute-done.8 = f32[3,3,128,128]{3,2,1,0:T(8,128)} collective-permute-done((f32[3,3,128,128]{3,2,1,0:T(8,128)}, f32[3,3,128,128]{3,2,1,0:T(8,128)}, u32[]{:S(2)}, u32[]{:S(2)}) %collective-permute-start.8) | collective-permute-done | bytes 589856 | tf_op jit(solution)/shard_map/ppermute | solution.py:26
  126.3 288.9 %while.13 = (s32[]{:T(128)}, f32[16,3,128,128]{3,2,1,0:T(8,128)}, f32[16,3,128,128]{3,2,1,0:T(8,128)}, s32[16,16]{1,0:T(8,128)S(1)}, f32[3,48,128,128]{3,2,1,0:T...) while((s32[]{:T(128)}, f32[16,3,128,128]{3,2,1,0:T(8,128)}, ...), condition=%wide.region_2.3_spmd.clone, body=%wide.region_1.2_spmd.clone.sunk | while | flops 1212679424 | bytes 26220016 | solution.py:46
  132.4 6.2 %select_add_fusion.4 = f32[16,3,128,128]{3,2,1,0:T(8,128)} fusion(f32[16,3,128,128]{3,2,1,0:T(8,128)} %get-tuple-element.149, f32[16,3,128,128]{3,2,1,0:T(8,128)} %gather_fusion, pred[16]{0:T(512)(128)(4,1)S(1)} %get-tuple-element.137, pred[]{:T(512)S(6)} %compare.18, f32[16,16,128,128]{3,2,1,0:T(8,128)} %get-tuple-element.162, s32[]{:T(128)} %get-tuple-element.148), kind=kOutput, calls=%fused_computation.5.clone.1 | convolution fusion | flops 1210318848 | bytes 10486289 | tf_op jit(solution)/shard_map/while/body/eval_jaxpr/akij,kjl->kail/dot_general | solution.py:41
  148.2 6.7 %select_add_fusion.4 = f32[16,3,128,128]{3,2,1,0:T(8,128)} fusion(f32[16,3,128,128]{3,2,1,0:T(8,128)} %get-tuple-element.149, f32[16,3,128,128]{3,2,1,0:T(8,128)} %gather_fusion, pred[16]{0:T(512)(128)(4,1)S(1)} %get-tuple-element.137, pred[]{:T(512)S(6)} %compare.18, f32[16,16,128,128]{3,2,1,0:T(8,128)} %get-tuple-element.162, s32[]{:T(128)} %get-tuple-element.148), kind=kOutput, calls=%fused_computation.5.clone.1 | convolution fusion | flops 1210318848 | bytes 10486289 | tf_op jit(solution)/shard_map/while/body/eval_jaxpr/akij,kjl->kail/dot_general | solution.py:41
  166.4 6.7 %select_add_fusion.4 = f32[16,3,128,128]{3,2,1,0:T(8,128)} fusion(f32[16,3,128,128]{3,2,1,0:T(8,128)} %get-tuple-element.149, f32[16,3,128,128]{3,2,1,0:T(8,128)} %gather_fusion, pred[16]{0:T(512)(128)(4,1)S(1)} %get-tuple-element.137, pred[]{:T(512)S(6)} %compare.18, f32[16,16,128,128]{3,2,1,0:T(8,128)} %get-tuple-element.162, s32[]{:T(128)} %get-tuple-element.148), kind=kOutput, calls=%fused_computation.5.clone.1 | convolution fusion | flops 1210318848 | bytes 10486289 | tf_op jit(solution)/shard_map/while/body/eval_jaxpr/akij,kjl->kail/dot_general | solution.py:41
  184.6 6.7 %select_add_fusion.4 = f32[16,3,128,128]{3,2,1,0:T(8,128)} fusion(f32[16,3,128,128]{3,2,1,0:T(8,128)} %get-tuple-element.149, f32[16,3,128,128]{3,2,1,0:T(8,128)} %gather_fusion, pred[16]{0:T(512)(128)(4,1)S(1)} %get-tuple-element.137, pred[]{:T(512)S(6)} %compare.18, f32[16,16,128,128]{3,2,1,0:T(8,128)} %get-tuple-element.162, s32[]{:T(128)} %get-tuple-element.148), kind=kOutput, calls=%fused_computation.5.clone.1 | convolution fusion | flops 1210318848 | bytes 10486289 | tf_op jit(solution)/shard_map/while/body/eval_jaxpr/akij,kjl->kail/dot_general | solution.py:41
  202.8 6.7 %select_add_fusion.4 = f32[16,3,128,128]{3,2,1,0:T(8,128)} fusion(f32[16,3,128,128]{3,2,1,0:T(8,128)} %get-tuple-element.149, f32[16,3,128,128]{3,2,1,0:T(8,128)} %gather_fusion, pred[16]{0:T(512)(128)(4,1)S(1)} %get-tuple-element.137, pred[]{:T(512)S(6)} %compare.18, f32[16,16,128,128]{3,2,1,0:T(8,128)} %get-tuple-element.162, s32[]{:T(128)} %get-tuple-element.148), kind=kOutput, calls=%fused_computation.5.clone.1 | convolution fusion | flops 1210318848 | bytes 10486289 | tf_op jit(solution)/shard_map/while/body/eval_jaxpr/akij,kjl->kail/dot_general | solution.py:41
  221.0 6.7 %select_add_fusion.4 = f32[16,3,128,128]{3,2,1,0:T(8,128)} fusion(f32[16,3,128,128]{3,2,1,0:T(8,128)} %get-tuple-element.149, f32[16,3,128,128]{3,2,1,0:T(8,128)} %gather_fusion, pred[16]{0:T(512)(128)(4,1)S(1)} %get-tuple-element.137, pred[]{:T(512)S(6)} %compare.18, f32[16,16,128,128]{3,2,1,0:T(8,128)} %get-tuple-element.162, s32[]{:T(128)} %get-tuple-element.148), kind=kOutput, calls=%fused_computation.5.clone.1 | convolution fusion | flops 1210318848 | bytes 10486289 | tf_op jit(solution)/shard_map/while/body/eval_jaxpr/akij,kjl->kail/dot_general | solution.py:41
  239.2 6.7 %select_add_fusion.4 = f32[16,3,128,128]{3,2,1,0:T(8,128)} fusion(f32[16,3,128,128]{3,2,1,0:T(8,128)} %get-tuple-element.149, f32[16,3,128,128]{3,2,1,0:T(8,128)} %gather_fusion, pred[16]{0:T(512)(128)(4,1)S(1)} %get-tuple-element.137, pred[]{:T(512)S(6)} %compare.18, f32[16,16,128,128]{3,2,1,0:T(8,128)} %get-tuple-element.162, s32[]{:T(128)} %get-tuple-element.148), kind=kOutput, calls=%fused_computation.5.clone.1 | convolution fusion | flops 1210318848 | bytes 10486289 | tf_op jit(solution)/shard_map/while/body/eval_jaxpr/akij,kjl->kail/dot_general | solution.py:41
  257.4 6.7 %select_add_fusion.4 = f32[16,3,128,128]{3,2,1,0:T(8,128)} fusion(f32[16,3,128,128]{3,2,1,0:T(8,128)} %get-tuple-element.149, f32[16,3,128,128]{3,2,1,0:T(8,128)} %gather_fusion, pred[16]{0:T(512)(128)(4,1)S(1)} %get-tuple-element.137, pred[]{:T(512)S(6)} %compare.18, f32[16,16,128,128]{3,2,1,0:T(8,128)} %get-tuple-element.162, s32[]{:T(128)} %get-tuple-element.148), kind=kOutput, calls=%fused_computation.5.clone.1 | convolution fusion | flops 1210318848 | bytes 10486289 | tf_op jit(solution)/shard_map/while/body/eval_jaxpr/akij,kjl->kail/dot_general | solution.py:41
  275.6 6.7 %select_add_fusion.4 = f32[16,3,128,128]{3,2,1,0:T(8,128)} fusion(f32[16,3,128,128]{3,2,1,0:T(8,128)} %get-tuple-element.149, f32[16,3,128,128]{3,2,1,0:T(8,128)} %gather_fusion, pred[16]{0:T(512)(128)(4,1)S(1)} %get-tuple-element.137, pred[]{:T(512)S(6)} %compare.18, f32[16,16,128,128]{3,2,1,0:T(8,128)} %get-tuple-element.162, s32[]{:T(128)} %get-tuple-element.148), kind=kOutput, calls=%fused_computation.5.clone.1 | convolution fusion | flops 1210318848 | bytes 10486289 | tf_op jit(solution)/shard_map/while/body/eval_jaxpr/akij,kjl->kail/dot_general | solution.py:41
  293.8 6.7 %select_add_fusion.4 = f32[16,3,128,128]{3,2,1,0:T(8,128)} fusion(f32[16,3,128,128]{3,2,1,0:T(8,128)} %get-tuple-element.149, f32[16,3,128,128]{3,2,1,0:T(8,128)} %gather_fusion, pred[16]{0:T(512)(128)(4,1)S(1)} %get-tuple-element.137, pred[]{:T(512)S(6)} %compare.18, f32[16,16,128,128]{3,2,1,0:T(8,128)} %get-tuple-element.162, s32[]{:T(128)} %get-tuple-element.148), kind=kOutput, calls=%fused_computation.5.clone.1 | convolution fusion | flops 1210318848 | bytes 10486289 | tf_op jit(solution)/shard_map/while/body/eval_jaxpr/akij,kjl->kail/dot_general | solution.py:41
  312.0 6.7 %select_add_fusion.4 = f32[16,3,128,128]{3,2,1,0:T(8,128)} fusion(f32[16,3,128,128]{3,2,1,0:T(8,128)} %get-tuple-element.149, f32[16,3,128,128]{3,2,1,0:T(8,128)} %gather_fusion, pred[16]{0:T(512)(128)(4,1)S(1)} %get-tuple-element.137, pred[]{:T(512)S(6)} %compare.18, f32[16,16,128,128]{3,2,1,0:T(8,128)} %get-tuple-element.162, s32[]{:T(128)} %get-tuple-element.148), kind=kOutput, calls=%fused_computation.5.clone.1 | convolution fusion | flops 1210318848 | bytes 10486289 | tf_op jit(solution)/shard_map/while/body/eval_jaxpr/akij,kjl->kail/dot_general | solution.py:41
  330.2 6.7 %select_add_fusion.4 = f32[16,3,128,128]{3,2,1,0:T(8,128)} fusion(f32[16,3,128,128]{3,2,1,0:T(8,128)} %get-tuple-element.149, f32[16,3,128,128]{3,2,1,0:T(8,128)} %gather_fusion, pred[16]{0:T(512)(128)(4,1)S(1)} %get-tuple-element.137, pred[]{:T(512)S(6)} %compare.18, f32[16,16,128,128]{3,2,1,0:T(8,128)} %get-tuple-element.162, s32[]{:T(128)} %get-tuple-element.148), kind=kOutput, calls=%fused_computation.5.clone.1 | convolution fusion | flops 1210318848 | bytes 10486289 | tf_op jit(solution)/shard_map/while/body/eval_jaxpr/akij,kjl->kail/dot_general | solution.py:41
  348.4 6.7 %select_add_fusion.4 = f32[16,3,128,128]{3,2,1,0:T(8,128)} fusion(f32[16,3,128,128]{3,2,1,0:T(8,128)} %get-tuple-element.149, f32[16,3,128,128]{3,2,1,0:T(8,128)} %gather_fusion, pred[16]{0:T(512)(128)(4,1)S(1)} %get-tuple-element.137, pred[]{:T(512)S(6)} %compare.18, f32[16,16,128,128]{3,2,1,0:T(8,128)} %get-tuple-element.162, s32[]{:T(128)} %get-tuple-element.148), kind=kOutput, calls=%fused_computation.5.clone.1 | convolution fusion | flops 1210318848 | bytes 10486289 | tf_op jit(solution)/shard_map/while/body/eval_jaxpr/akij,kjl->kail/dot_general | solution.py:41
  366.6 6.7 %select_add_fusion.4 = f32[16,3,128,128]{3,2,1,0:T(8,128)} fusion(f32[16,3,128,128]{3,2,1,0:T(8,128)} %get-tuple-element.149, f32[16,3,128,128]{3,2,1,0:T(8,128)} %gather_fusion, pred[16]{0:T(512)(128)(4,1)S(1)} %get-tuple-element.137, pred[]{:T(512)S(6)} %compare.18, f32[16,16,128,128]{3,2,1,0:T(8,128)} %get-tuple-element.162, s32[]{:T(128)} %get-tuple-element.148), kind=kOutput, calls=%fused_computation.5.clone.1 | convolution fusion | flops 1210318848 | bytes 10486289 | tf_op jit(solution)/shard_map/while/body/eval_jaxpr/akij,kjl->kail/dot_general | solution.py:41
  384.8 6.7 %select_add_fusion.4 = f32[16,3,128,128]{3,2,1,0:T(8,128)} fusion(f32[16,3,128,128]{3,2,1,0:T(8,128)} %get-tuple-element.149, f32[16,3,128,128]{3,2,1,0:T(8,128)} %gather_fusion, pred[16]{0:T(512)(128)(4,1)S(1)} %get-tuple-element.137, pred[]{:T(512)S(6)} %compare.18, f32[16,16,128,128]{3,2,1,0:T(8,128)} %get-tuple-element.162, s32[]{:T(128)} %get-tuple-element.148), kind=kOutput, calls=%fused_computation.5.clone.1 | convolution fusion | flops 1210318848 | bytes 10486289 | tf_op jit(solution)/shard_map/while/body/eval_jaxpr/akij,kjl->kail/dot_general | solution.py:41
  403.1 6.7 %select_add_fusion.4 = f32[16,3,128,128]{3,2,1,0:T(8,128)} fusion(f32[16,3,128,128]{3,2,1,0:T(8,128)} %get-tuple-element.149, f32[16,3,128,128]{3,2,1,0:T(8,128)} %gather_fusion, pred[16]{0:T(512)(128)(4,1)S(1)} %get-tuple-element.137, pred[]{:T(512)S(6)} %compare.18, f32[16,16,128,128]{3,2,1,0:T(8,128)} %get-tuple-element.162, s32[]{:T(128)} %get-tuple-element.148), kind=kOutput, calls=%fused_computation.5.clone.1 | convolution fusion | flops 1210318848 | bytes 10486289 | tf_op jit(solution)/shard_map/while/body/eval_jaxpr/akij,kjl->kail/dot_general | solution.py:41
  415.2 9.0 %convolution_bitcast_fusion = f32[16,128,128]{2,1,0:T(8,128)} fusion(f32[16,3,128,128]{3,2,1,0:T(8,128)} %get-tuple-element.41, f32[16,3,128,128]{3,2,1,0:T(8,128)} %get-tuple-element.40), kind=kOutput, calls=%fused_computation.24 | convolution fusion | flops 1207959552 | bytes 7340032 | tf_op jit(solution)/shard_map/kaij,kail->kjl/dot_general | solution.py:54
  428.4 120.4 %all-reduce.2.cloned.1.call-done = f32[16,128,128]{2,1,0:T(8,128)} async-done(((f32[16,128,128]{2,1,0:T(8,128)}), f32[16,128,128]{2,1,0:T(8,128)}) %all-reduce.2.cloned.1.call-update) | async-done | bytes 1048592 | tf_op jit(solution)/shard_map/psum | solution.py:59
  (211 shorter events, 261.4 us)
Async XLA Ops:
  7.2 82.3 %copy-start.1 = (f32[3,3,128,128]{3,2,1,0:T(8,128)S(1)}, f32[3,3,128,128]{3,2,1,0:T(8,128)}, u32[]{:S(2)}) copy-start(f32[3,3,128,128]{3,2,1,0:T(8,128)} %param.6) | copy-start | bytes 1769476
  7.2 119.1 %all-gather.2.cloned.1.call-start = ((), (), s32[]{:S(2)}) async-start(), calls=%async_computation | async-start | bytes 17825792 | tf_op jit(solution)/shard_map/all_gather | solution.py:49
  12.8 536.0 %all-reduce.2.cloned.1.call-start = ((), (), s32[]{:S(2)}) async-start(), calls=%async_computation.1 | async-start | bytes 2097152 | tf_op jit(solution)/shard_map/psum | solution.py:59
  12.9 17.1 %collective-permute-start = (f32[3,3,128,128]{3,2,1,0:T(8,128)}, f32[3,3,128,128]{3,2,1,0:T(8,128)S(1)}, u32[]{:S(2)}, u32[]{:S(2)}) collective-permute-start(f32[3,3,128,128]{3,2,1,0:T(8,128)} %param.6), channel_id=1, source_target_pairs={{0,1},{1,2},{2,3},{3,4},{4,5},{5,6},{6,7},{7,8},{8,9},{9,10},{10,1... | collective-permute-start | bytes 1769480 | tf_op jit(solution)/shard_map/ppermute | solution.py:26
  15.0 15.0 %collective-permute-start.1 = (f32[3,3,128,128]{3,2,1,0:T(8,128)}, f32[3,3,128,128]{3,2,1,0:T(8,128)S(1)}, u32[]{:S(2)}, u32[]{:S(2)}) collective-permute-start(f32[3,3,128,128]{3,2,1,0:T(8,128)} %param.6), channel_id=1, source_target_pairs={{0,15},{1,0},{2,1},{3,2},{4,3},{5,4},{6,5},{7,6},{8,7},{9,8},{10,9... | collective-permute-start | bytes 1769480 | tf_op jit(solution)/shard_map/ppermute | solution.py:29
  30.0 15.0 %collective-permute-start.2 = (f32[3,3,128,128]{3,2,1,0:T(8,128)S(1)}, f32[3,3,128,128]{3,2,1,0:T(8,128)S(1)}, u32[]{:S(2)}, u32[]{:S(2)}) collective-permute-start(f32[3,3,128,128]{3,2,1,0:T(8,128)S(1)} %collective-permute-done), channel_id=1, source_target_pairs={{0,1},{1,2},{2,3},{3,4},{4,5},{5,6},{6,7},{7,8},{8,9},{9,10},{10,1... | collective-permute-start | bytes 1769480 | tf_op jit(solution)/shard_map/ppermute | solution.py:26
  30.0 47.1 %copy-start.8 = (f32[3,3,128,128]{3,2,1,0:T(8,128)}, f32[3,3,128,128]{3,2,1,0:T(8,128)S(1)}, u32[]{:S(2)}) copy-start(f32[3,3,128,128]{3,2,1,0:T(8,128)S(1)} %collective-permute-done.1) | copy-start | bytes 1769476
  30.0 15.0 %collective-permute-start.3 = (f32[3,3,128,128]{3,2,1,0:T(8,128)S(1)}, f32[3,3,128,128]{3,2,1,0:T(8,128)S(1)}, u32[]{:S(2)}, u32[]{:S(2)}) collective-permute-start(f32[3,3,128,128]{3,2,1,0:T(8,128)S(1)} %collective-permute-done.1), channel_id=1, source_target_pairs={{0,15},{1,0},{2,1},{3,2},{4,3},{5,4},{6,5},{7,6},{8,7},{9,8},{10,9... | collective-permute-start | bytes 1769480 | tf_op jit(solution)/shard_map/ppermute | solution.py:29
  45.0 32.1 %copy-start.10 = (f32[3,3,128,128]{3,2,1,0:T(8,128)}, f32[3,3,128,128]{3,2,1,0:T(8,128)S(1)}, u32[]{:S(2)}) copy-start(f32[3,3,128,128]{3,2,1,0:T(8,128)S(1)} %collective-permute-done.2) | copy-start | bytes 1769476
  45.0 14.0 %collective-permute-start.4 = (f32[3,3,128,128]{3,2,1,0:T(8,128)S(1)}, f32[3,3,128,128]{3,2,1,0:T(8,128)S(1)}, u32[]{:S(2)}, u32[]{:S(2)}) collective-permute-start(f32[3,3,128,128]{3,2,1,0:T(8,128)S(1)} %collective-permute-done.2), channel_id=1, source_target_pairs={{0,1},{1,2},{2,3},{3,4},{4,5},{5,6},{6,7},{7,8},{8,9},{9,10},{10,1... | collective-permute-start | bytes 1769480 | tf_op jit(solution)/shard_map/ppermute | solution.py:26
  45.0 27.3 %copy-start.4 = (f32[3,3,128,128]{3,2,1,0:T(8,128)}, f32[3,3,128,128]{3,2,1,0:T(8,128)S(1)}, u32[]{:S(2)}) copy-start(f32[3,3,128,128]{3,2,1,0:T(8,128)S(1)} %collective-permute-done.3) | copy-start | bytes 1769476
  45.0 14.0 %collective-permute-start.5 = (f32[3,3,128,128]{3,2,1,0:T(8,128)S(1)}, f32[3,3,128,128]{3,2,1,0:T(8,128)S(1)}, u32[]{:S(2)}, u32[]{:S(2)}) collective-permute-start(f32[3,3,128,128]{3,2,1,0:T(8,128)S(1)} %collective-permute-done.3), channel_id=1, source_target_pairs={{0,15},{1,0},{2,1},{3,2},{4,3},{5,4},{6,5},{7,6},{8,7},{9,8},{10,9... | collective-permute-start | bytes 1769480 | tf_op jit(solution)/shard_map/ppermute | solution.py:29
  59.0 13.2 %collective-permute-start.6 = (f32[3,3,128,128]{3,2,1,0:T(8,128)S(1)}, f32[3,3,128,128]{3,2,1,0:T(8,128)}, u32[]{:S(2)}, u32[]{:S(2)}) collective-permute-start(f32[3,3,128,128]{3,2,1,0:T(8,128)S(1)} %collective-permute-done.4), channel_id=1, source_target_pairs={{0,1},{1,2},{2,3},{3,4},{4,5},{5,6},{6,7},{7,8},{8,9},{9,10},{10,1... | collective-permute-start | bytes 1769480 | tf_op jit(solution)/shard_map/ppermute | solution.py:26
  59.0 13.2 %collective-permute-start.7 = (f32[3,3,128,128]{3,2,1,0:T(8,128)S(1)}, f32[3,3,128,128]{3,2,1,0:T(8,128)}, u32[]{:S(2)}, u32[]{:S(2)}) collective-permute-start(f32[3,3,128,128]{3,2,1,0:T(8,128)S(1)} %collective-permute-done.5), channel_id=1, source_target_pairs={{0,15},{1,0},{2,1},{3,2},{4,3},{5,4},{6,5},{7,6},{8,7},{9,8},{10,9... | collective-permute-start | bytes 1769480 | tf_op jit(solution)/shard_map/ppermute | solution.py:29
  72.3 12.4 %collective-permute-start.8 = (f32[3,3,128,128]{3,2,1,0:T(8,128)}, f32[3,3,128,128]{3,2,1,0:T(8,128)}, u32[]{:S(2)}, u32[]{:S(2)}) collective-permute-start(f32[3,3,128,128]{3,2,1,0:T(8,128)} %collective-permute-done.6), channel_id=1, source_target_pairs={{0,1},{1,2},{2,3},{3,4},{4,5},{5,6},{6,7},{7,8},{8,9},{9,10},{10,1... | collective-permute-start | bytes 1769480 | tf_op jit(solution)/shard_map/ppermute | solution.py:26
  72.3 20.7 %collective-permute-start.9 = (f32[3,3,128,128]{3,2,1,0:T(8,128)}, f32[3,3,128,128]{3,2,1,0:T(8,128)S(1)}, u32[]{:S(2)}, u32[]{:S(2)}) collective-permute-start(f32[3,3,128,128]{3,2,1,0:T(8,128)} %collective-permute-done.7), channel_id=1, source_target_pairs={{0,15},{1,0},{2,1},{3,2},{4,3},{5,4},{6,5},{7,6},{8,7},{9,8},{10,9... | collective-permute-start | bytes 1769480 | tf_op jit(solution)/shard_map/ppermute | solution.py:29
  77.9 19.8 %copy-start.5 = (f32[3,3,128,128]{3,2,1,0:T(8,128)S(1)}, f32[3,3,128,128]{3,2,1,0:T(8,128)}, u32[]{:S(2)}) copy-start(f32[3,3,128,128]{3,2,1,0:T(8,128)} %copy-done.4) | copy-start | bytes 1769476
  77.9 21.5 %copy-start.3 = (f32[3,3,128,128]{3,2,1,0:T(8,128)S(1)}, f32[3,3,128,128]{3,2,1,0:T(8,128)}, u32[]{:S(2)}) copy-start(f32[3,3,128,128]{3,2,1,0:T(8,128)} %copy-done.2) | copy-start | bytes 1769476
  84.6 14.0 %collective-permute-start.10 = (f32[3,3,128,128]{3,2,1,0:T(8,128)}, f32[3,3,128,128]{3,2,1,0:T(8,128)S(1)}, u32[]{:S(2)}, u32[]{:S(2)}) collective-permute-start(f32[3,3,128,128]{3,2,1,0:T(8,128)} %collective-permute-done.8), channel_id=1, source_target_pairs={{0,1},{1,2},{2,3},{3,4},{4,5},{5,6},{6,7},{7,8},{8,9},{9,10},{10,1... | collective-permute-start | bytes 1769480 | tf_op jit(solution)/shard_map/ppermute | solution.py:26
  92.9 11.6 %collective-permute-start.11 = (f32[3,3,128,128]{3,2,1,0:T(8,128)S(1)}, f32[3,3,128,128]{3,2,1,0:T(8,128)S(1)}, u32[]{:S(2)}, u32[]{:S(2)}) collective-permute-start(f32[3,3,128,128]{3,2,1,0:T(8,128)S(1)} %collective-permute-done.9), channel_id=1, source_target_pairs={{0,15},{1,0},{2,1},{3,2},{4,3},{5,4},{6,5},{7,6},{8,7},{9,8},{10,9... | collective-permute-start | bytes 1769480 | tf_op jit(solution)/shard_map/ppermute | solution.py:29
  98.6 13.1 %collective-permute-start.12 = (f32[3,3,128,128]{3,2,1,0:T(8,128)S(1)}, f32[3,3,128,128]{3,2,1,0:T(8,128)S(1)}, u32[]{:S(2)}, u32[]{:S(2)}) collective-permute-start(f32[3,3,128,128]{3,2,1,0:T(8,128)S(1)} %collective-permute-done.10), channel_id=1, source_target_pairs={{0,1},{1,2},{2,3},{3,4},{4,5},{5,6},{6,7},{7,8},{8,9},{9,10},{10,1... | collective-permute-start | bytes 1769480 | tf_op jit(solution)/shard_map/ppermute | solution.py:26
  104.6 14.4 %collective-permute-start.13 = (f32[3,3,128,128]{3,2,1,0:T(8,128)S(1)}, f32[3,3,128,128]{3,2,1,0:T(8,128)S(1)}, u32[]{:S(2)}, u32[]{:S(2)}) collective-permute-start(f32[3,3,128,128]{3,2,1,0:T(8,128)S(1)} %collective-permute-done.11), channel_id=1, source_target_pairs={{0,15},{1,0},{2,1},{3,2},{4,3},{5,4},{6,5},{7,6},{8,7},{9,8},{10,9... | collective-permute-start | bytes 1769480 | tf_op jit(solution)/shard_map/ppermute | solution.py:29
  111.8 13.6 %collective-permute-start.14 = (f32[3,3,128,128]{3,2,1,0:T(8,128)S(1)}, f32[3,3,128,128]{3,2,1,0:T(8,128)S(1)}, u32[]{:S(2)}, u32[]{:S(2)}) collective-permute-start(f32[3,3,128,128]{3,2,1,0:T(8,128)S(1)} %collective-permute-done.12), channel_id=1, source_target_pairs={{0,1},{1,2},{2,3},{3,4},{4,5},{5,6},{6,7},{7,8},{8,9},{9,10},{10,1... | collective-permute-start | bytes 1769480 | tf_op jit(solution)/shard_map/ppermute | solution.py:26
  126.3 297.9 %copy-start.12 = (s32[16,16]{1,0:T(8,128)S(1)}, s32[16,16]{1,0:T(8,128)}, u32[]{:S(2)}) copy-start(s32[16,16]{1,0:T(8,128)} %param.9) | copy-start | bytes 3076
  (6 other events, 69.3 us)
Sparse Core Ops, SparseCore 0:
  12.9 99.6 all-gather.1
  424.3 124.4 all-reduce.1
